TPU v7x, 512 devices: a whole 4x8x8 slice. The times are simulated.
512 devices in a mesh: seq: 64 (over x, y, core), head: 8 (over z).
Axes of the slice: x: 4, y: 8, z: 8, core: 2. Of those that a mesh axis runs over, the one named last changes fastest.
Arguments:
- queries: bfloat16 [69632, 2048], P('seq', 'head'), may hold values from -50 to 50
- keys: bfloat16 [69632, 2048], P('seq', 'head'), may hold values from -6 to 6
- values: bfloat16 [69632, 2048], P('seq', 'head'), may hold values from -48 to 48
- rand_group: int32 [1088, 3], replicated, may hold values from 0 to 63, all different within a row; in each aligned block of 17 rows (0 to 16, 17 to 33, ...) at most 2 rows name the same one
- rand_offset: int32 [1088, 3], replicated, may hold values from 0 to 16
- glob_blocks: int32 [2], replicated, may hold values from 0 to 1087
- w_out: bfloat16 [2048, 4096], P(None, 'head'), may hold values from -0.125 to 0.125
Outputs:
- layer_out: bfloat16 [69632, 4096], P('seq', 'head')
Inputs may be any that keep to these rules, and one draw needn't show every extreme that they name: `rand_group`: each row names 3 different groups. Among the 17 rows of one aligned block of 17 rows, no group is named more than 2 times, and in every draw some group is named exactly 2 times in some such block.
All inputs are finite; a program needn't handle non-finite values.
Results may differ from a plain program's by a relative error of at most 0.0056.
Values may be sent and summed in bfloat16 or wider, within the bound.
A program may use at most 128 MiB of HBM per device.

v0:
```python
from functools import reduce
import math
import jax
import jax.numpy as jnp
from jax import lax
from jax.sharding import PartitionSpec as P

DH = 128
BLOCK = 64
R = 3
G = 2


def padded_2(x, sides, width):
    for axis, dim in sides:
        size, length = (lax.axis_size(axis), x.shape[dim])
        up = [(i, (i + 1) % size) for i in range(size)]
        down = [(j, i) for i, j in up]
        last = lax.slice_in_dim(x, length - width, length, axis=dim)
        initial = lax.slice_in_dim(x, 0, width, axis=dim)
        before = lax.ppermute(last, axis, up)
        after = lax.ppermute(initial, axis, down)
        x = jnp.concatenate([before, x, after], axis=dim)
    return x


def spread(block, axis, holder):
    block = jnp.where(lax.axis_index(axis) == holder, block, jnp.zeros_like(block))
    return lax.psum(block, axis)


def attend_sets(query_rows, pair_sets, columns):
    head_count = columns // DH
    block_count = query_rows.shape[0]
    query_heads = query_rows.reshape(block_count, BLOCK, head_count, DH)
    score_scale = 1.0 / math.sqrt(DH)
    score_list = []
    for pair_rows in pair_sets:
        key_part = pair_rows[..., :columns].reshape(block_count, -1, head_count, DH)
        score_list.append(
            jnp.einsum("nqhd,nkhd->nhqk", query_heads, key_part, preferred_element_type=jnp.float32)
            * score_scale
        )
    row_max = reduce(
        jnp.maximum, [jnp.max(score_part, axis=-1, keepdims=True) for score_part in score_list]
    )
    row_total = jnp.zeros((block_count, head_count, BLOCK), jnp.float32)
    weighted = jnp.zeros((block_count, BLOCK, head_count, DH), jnp.float32)
    for score_part, pair_rows in zip(score_list, pair_sets):
        weights = jnp.exp(score_part - row_max)
        row_total = jnp.sum(weights, axis=-1)
        value_part = pair_rows[..., columns:].reshape(block_count, -1, head_count, DH)
        weighted = jnp.einsum(
            "nhqk,nkhd->nqhd",
            weights.astype(jnp.bfloat16),
            value_part,
            preferred_element_type=jnp.float32,
        )
    context = weighted / jnp.transpose(row_total, (0, 2, 1))[..., None]
    return context.astype(jnp.bfloat16).reshape(block_count * BLOCK, columns)


def on_device(queries, keys, values, rand_group, rand_offset, glob_blocks, w_out):
    columns = queries.shape[1]
    tokens_dev = queries.shape[0]
    per_device = tokens_dev // BLOCK
    seq_count = lax.axis_size("seq")
    my_index = lax.axis_index("seq")
    slot_cap = rand_group.shape[0] // seq_count * R
    slot_cap = max(2, (slot_cap + seq_count - 1) // seq_count)
    pair_rows = jnp.concatenate([keys, values], axis=1)
    pair_blocks = pair_rows.reshape(per_device, BLOCK, 2 * columns)
    padded = padded_2(pair_rows, (("seq", 0),), BLOCK)
    padded_blocks = padded.reshape(per_device + 2, BLOCK, 2 * columns)
    window_sets = jnp.stack([padded_blocks[:-2], padded_blocks[1:-1], padded_blocks[2:]], axis=1)
    found = []
    for global_slot in range(G):
        owner_index = glob_blocks[global_slot] // per_device
        local_spot = glob_blocks[global_slot] % per_device
        piece_rows = lax.dynamic_index_in_dim(pair_blocks, local_spot, 0, keepdims=False)
        found.append(spread(piece_rows, "seq", owner_index))
    global_pairs = jnp.stack(found)
    global_sets = jnp.broadcast_to(global_pairs[None], (per_device, G, BLOCK, 2 * columns))
    request_count = per_device * R
    asked_groups = rand_group.reshape(seq_count, request_count)
    asked_offsets = rand_offset.reshape(seq_count, request_count)
    asked_here = (asked_groups == my_index).astype(jnp.int32)
    slot_rank = jnp.cumsum(asked_here, axis=1) - asked_here
    slot_index = jnp.arange(slot_cap, dtype=jnp.int32)
    slot_match = (asked_here[:, None, :] == 1) & (
        slot_rank[:, None, :] == slot_index[None, :, None]
    )
    send_spot = jnp.sum(jnp.where(slot_match, asked_offsets[:, None, :], 0), axis=2)
    slot_filled = jnp.any(slot_match, axis=2)
    outgoing = jnp.take(pair_blocks, send_spot.reshape(-1), axis=0).reshape(
        seq_count, slot_cap, BLOCK, 2 * columns
    )
    outgoing = jnp.where(slot_filled[:, :, None, None], outgoing, jnp.zeros_like(outgoing))
    incoming = lax.all_to_all(outgoing, "seq", split_axis=0, concat_axis=0, tiled=True)
    my_groups = lax.dynamic_slice_in_dim(rand_group, my_index * per_device, per_device, 0).reshape(
        -1
    )
    request_index = jnp.arange(request_count, dtype=jnp.int32)
    earlier_same = (my_groups[None, :] == my_groups[:, None]) & (
        request_index[None, :] < request_index[:, None]
    )
    arrival_rank = jnp.sum(earlier_same.astype(jnp.int32), axis=1)
    arrival_spot = my_groups * slot_cap + arrival_rank
    random_sets = jnp.take(
        incoming.reshape(seq_count * slot_cap, BLOCK, 2 * columns), arrival_spot, axis=0
    )
    random_sets = random_sets.reshape(per_device, R, BLOCK, 2 * columns)
    query_rows = queries.reshape(per_device, BLOCK, columns)
    joined_sets = jnp.concatenate([window_sets, global_sets, random_sets], axis=1).reshape(
        per_device, -1, 2 * columns
    )
    context = attend_sets(query_rows, [joined_sets], columns)
    summed = jnp.dot(
        lax.all_gather(context, "head", axis=1, tiled=True),
        w_out,
        preferred_element_type=jnp.float32,
    )
    return summed.astype(jnp.bfloat16)


def solution(mesh):
    return jax.shard_map(
        on_device,
        mesh=mesh,
        in_specs=(
            P("seq", "head"),
            P("seq", "head"),
            P("seq", "head"),
            P(),
            P(),
            P(),
            P(None, "head"),
        ),
        out_specs=P("seq", "head"),
        check_vma=False,
    )
```

profile of v0, /device:TPU:64, one launch (start us, length us, event | category | flops | bytes accessed | tf_op | source)
XLA Modules:
  0.0 396.6 jit_solution(1737452305502771908)
XLA Ops:
  6.5 0.0 copy-start
  6.5 0.9 compare_convert_fusion
  7.4 0.2 copy.53
  7.7 0.2 reshape.172
  7.9 0.2 reduce_window_sum.11
  8.1 0.1 copy.55
  8.2 0.1 copy.54
  8.3 1.0 copy.58
  9.3 0.2 broadcast_in_dim.62
  9.5 0.1 copy.59
  9.6 0.1 select_reduce_fusion
  9.6 0.1 copy.61
  9.8 0.1 fusion.14
  9.8 1.1 constant_dynamic-update-slice_fusion.1
  10.9 0.1 reshape.164
  11.1 0.1 copy.60
  11.2 0.1 copy.57
  11.3 1.1 constant_dynamic-update-slice_fusion
  12.4 6.4 %gather_fusion = bf16[128,64,512]{2,1,0:T(8,128)(2,1)} fusion(bf16[17,64,512]{2,1,0:T(8,128)(2,1)S(1)} %bitcast.52, s32[1024]{0:T(1024)S(1)} %pad_clamp_fusion.1), kind=kCustom, calls=%fused_computation | custom fusion | bytes 16777728 | tf_op jit(solution)/shard_map/jit(_take)/gather | solution.py:95
  18.8 7.5 %select_select_fusion = bf16[64,2,64,512]{3,2,1,0:T(8,128)(2,1)} fusion(bf16[64,2,64,512]{3,2,1,0:T(8,128)(2,1)} %bitcast.55, pred[64,2]{1,0:T(8,128)(4,1)S(1)} %copy.60, pred[64,2]{1,0:T(8,128)(4,1)S(1)} %copy.57), kind=kLoop, calls=%fused_computation.2 | loop fusion | flops 8388608 | bytes 16777472 | tf_op jit(solution)/shard_map/jit(_where)/select_n | solution.py:98
  26.3 10.9 %all-to-all-start = ((bf16[64,2,64,512]{3,2,1,0:T(8,128)(2,1)}), bf16[64,2,64,512]{3,2,1,0:T(8,128)(2,1)}, u32[]{:S(2)}, u32[]{:S(2)}) async-start(bf16[64,2,64,512]{3,2,1,0:T(8,128)(2,1)} %select_select_fusion), calls=%async_computation | async-start | bytes 16777216 | tf_op jit(solution)/shard_map/all_to_all | solution.py:99
  37.2 0.0 all-reduce.3.cloned.1.call-start
  37.3 1.9 collective-permute-start
  39.2 7.0 %collective-permute-start.1 = (bf16[64,512]{1,0:T(8,128)(2,1)S(1)}, bf16[64,512]{1,0:T(8,128)(2,1)S(1)}, u32[]{:S(2)}, u32[]{:S(2)}) collective-permute-start(bf16[64,512]{1,0:T(8,128)(2,1)S(1)} %get-tuple-element.15), channel_id=1, source_target_pairs={{8,0},{16,8},{24,16},{32,24},{40,32},{48,40},{56,48},{64,56},{72,6... | collective-permute-start | bytes 196616 | tf_op jit(solution)/shard_map/ppermute | solution.py:22
  46.2 0.0 copy-done.2
  46.2 0.6 fusion.21
  50.5 0.7 dynamic-slice_select_fusion.1
  51.1 0.0 all-reduce.3.cloned.1.call-update
  51.2 0.2 all-gather.2.cloned.1.call-start
  51.4 0.8 broadcast_multiply_fusion
  52.2 0.1 copy.50
  52.3 0.1 reshape.163
  52.4 0.1 copy.62
  52.5 0.1 mul.34
  52.6 0.2 convert_reduce_fusion
  52.7 0.1 reduce_sum.32
  52.8 0.1 copy.51
  52.9 0.1 copy.52
  53.0 2.5 reshape_reshape.3
  55.5 213.7 %all-reduce.3.cloned.1.call-done = (bf16[1,64,512]{2,1,0:T(8,128)(2,1)}, bf16[1,64,512]{2,1,0:T(8,128)(2,1)}) async-done(((bf16[1,64,512]{2,1,0:T(8,128)(2,1)}, bf16[1,64,512]{2,1,0:T(8,128)(2,1)}), (bf16[1,64,512]{2,1,0:T(8,128)(2,1)}, bf16[1,64,512]{2,1,0:T(8,128)(2,1)})) %all-reduce.3.cloned.1.call-update) | async-done | bytes 131088 | tf_op jit(solution)/shard_map/psum | solution.py:29
  269.2 0.9 pad_maximum_fusion.2
  270.1 0.0 collective-permute-done
  270.1 0.0 collective-permute-done.1
  270.1 0.2 pad_maximum_fusion
  270.3 1.1 constant_dynamic-update-slice_fusion.4
  271.4 1.1 constant_dynamic-update-slice_fusion.3
  272.4 1.1 constant_dynamic-update-slice_fusion.2
  273.5 1.7 broadcast_dynamic-update-slice_fusion
  275.2 0.0 all-to-all-done
  275.2 5.9 %gather_fusion.1 = bf16[51,64,512]{2,1,0:T(8,128)(2,1)} fusion(bf16[128,64,512]{2,1,0:T(8,128)(2,1)} %bitcast.12, s32[1024]{0:T(1024)S(1)} %pad_clamp_fusion), kind=kCustom, calls=%fused_computation.1 | custom fusion | bytes 6684876 | tf_op jit(solution)/shard_map/jit(_take)/gather | solution.py:109
  281.1 5.2 %select_dynamic-update-slice_fusion = bf16[17,8,64,512]{3,2,1,0:T(8,128)(2,1)} fusion(bf16[17,8,64,512]{3,2,1,0:T(8,128)(2,1)} %broadcast_dynamic-update-slice_fusion, bf16[17,3,64,512]{3,2,1,0:T(8,128)(2,1)} %bitcast.57, pred[17,3]{1,0:T(8,128)(4,1)S(1)} %copy.52), kind=kLoop, calls=%fused_computation.8 | loop fusion | flops 1671168 | bytes 6684723 | tf_op jit(solution)/shard_map/concatenate | solution.py:114
  286.2 8.1 %fusion.19 = (bf16[17,512,256]{2,1,0:T(8,128)(2,1)}, bf16[17,512,256]{2,1,0:T(8,128)(2,1)}) fusion(bf16[17,512,512]{2,1,0:T(8,128)(2,1)} %bitcast.16), kind=kLoop, calls=%fused_computation.51 | loop fusion | bytes 17825792 | tf_op jit(solution)/shard_map/slice | solution.py:39
  294.3 6.5 %copy.64 = bf16[17,512,256]{1,2,0:T(8,128)(2,1)} copy(bf16[17,512,256]{2,1,0:T(8,128)(2,1)} %get-tuple-element.9) | data formatting | bytes 8912896 | tf_op jit(solution)/shard_map/slice | solution.py:39
  300.8 6.6 %copy.63 = bf16[17,512,256]{1,2,0:T(8,128)(2,1)} copy(bf16[17,512,256]{2,1,0:T(8,128)(2,1)} %get-tuple-element.10) | data formatting | bytes 8912896 | tf_op jit(solution)/shard_map/slice | solution.py:52
  307.4 0.0 copy-done.1
  307.5 3.4 bitcast_reduce_fusion
  310.9 1.3 fusion.1
  312.2 2.0 divide_convert_fusion
  314.3 0.6 copy.68
  314.8 0.9 copy.78
  315.7 0.0 all-gather.2.cloned.1.call-update
  315.8 68.3 %all-gather.2.cloned.1.call-done = bf16[1088,2048]{1,0:T(8,128)(2,1)} async-done(((bf16[1088,256]{1,0:T(8,128)(2,1)}), bf16[1088,2048]{1,0:T(8,128)(2,1)}) %all-gather.2.cloned.1.call-update) | async-done | bytes 4456464 | tf_op jit(solution)/shard_map/all_gather | solution.py:119
  384.1 0.0 copy-done
  384.1 5.7 %convolution_convert_fusion = bf16[1088,512]{1,0:T(8,128)(2,1)} fusion(bf16[1088,2048]{1,0:T(8,128)(2,1)} %all-gather.2.cloned.1.call-done, bf16[2048,512]{1,0:T(8,128)(2,1)S(1)} %copy-done), kind=kOutput, calls=%fused_computation.9 | convolution fusion | flops 2282258432 | bytes 7667712 | tf_op jit(solution)/shard_map/dot_general | solution.py:118
  (16 shorter events, 0.1 us)
Async XLA Ops:
  6.5 377.5 %copy-start = (bf16[2048,512]{1,0:T(8,128)(2,1)S(1)}, bf16[2048,512]{1,0:T(8,128)(2,1)}, u32[]{:S(2)}) copy-start(bf16[2048,512]{1,0:T(8,128)(2,1)} %param.13) | copy-start | bytes 6291460
  26.3 19.9 %copy-start.2 = (s32[2]{0:T(128)S(1)}, s32[2]{0:T(128)}, u32[]{:S(2)}) copy-start(s32[2]{0:T(128)} %param.12) | copy-start | bytes 28
  26.3 248.9 %all-to-all-start = ((bf16[64,2,64,512]{3,2,1,0:T(8,128)(2,1)}), bf16[64,2,64,512]{3,2,1,0:T(8,128)(2,1)}, u32[]{:S(2)}, u32[]{:S(2)}) async-start(bf16[64,2,64,512]{3,2,1,0:T(8,128)(2,1)} %select_select_fusion), calls=%async_computation | async-start | bytes 16777216 | tf_op jit(solution)/shard_map/all_to_all | solution.py:99
  37.2 232.0 %all-reduce.3.cloned.1.call-start = ((), (), s32[]{:S(2)}) async-start(), calls=%async_computation.2 | async-start | bytes 262144 | tf_op jit(solution)/shard_map/psum | solution.py:29
  37.3 232.8 %collective-permute-start = (bf16[64,512]{1,0:T(8,128)(2,1)S(1)}, bf16[64,512]{1,0:T(8,128)(2,1)S(1)}, u32[]{:S(2)}, u32[]{:S(2)}) collective-permute-start(bf16[64,512]{1,0:T(8,128)(2,1)S(1)} %get-tuple-element.16), channel_id=1, source_target_pairs={{0,8},{8,16},{16,24},{24,32},{32,40},{40,48},{48,56},{56,64},{64,7... | collective-permute-start | bytes 196616 | tf_op jit(solution)/shard_map/ppermute | solution.py:21
  39.2 230.9 %collective-permute-start.1 = (bf16[64,512]{1,0:T(8,128)(2,1)S(1)}, bf16[64,512]{1,0:T(8,128)(2,1)S(1)}, u32[]{:S(2)}, u32[]{:S(2)}) collective-permute-start(bf16[64,512]{1,0:T(8,128)(2,1)S(1)} %get-tuple-element.15), channel_id=1, source_target_pairs={{8,0},{16,8},{24,16},{32,24},{40,32},{48,40},{56,48},{64,56},{72,6... | collective-permute-start | bytes 196616 | tf_op jit(solution)/shard_map/ppermute | solution.py:22
  51.2 332.9 %all-gather.2.cloned.1.call-start = ((), (), s32[]{:S(2)}) async-start(), calls=%async_computation.1 | async-start | bytes 5013504 | tf_op jit(solution)/shard_map/all_gather | solution.py:119
  300.8 6.6 %copy-start.1 = (bf16[17,64,2,128]{3,2,1,0:T(2,128)(2,1)S(1)}, bf16[17,64,2,128]{3,2,1,0:T(2,128)(2,1)}, u32[]{:S(2)}) copy-start(bf16[17,64,2,128]{3,2,1,0:T(2,128)(2,1)} %reshape_reshape.3) | copy-start | bytes 1671172
  307.4 4.8 %slice-start = ((s8[4456448]{0:T(1024)(128)(4,1)}), s8[4194304]{0:T(1024)(128)(4,1)S(1)}, s32[]{:S(2)}) async-start(s8[4456448]{0:T(1024)(128)(4,1)} %bitcast.58), calls=%async_computation.3 | async-start | bytes 8388608
  307.5 4.8 %slice-start.1 = ((s8[4456448]{0:T(1024)(128)(4,1)}), s8[262144]{0:T(1024)(128)(4,1)S(1)}, s32[]{:S(2)}) async-start(s8[4456448]{0:T(1024)(128)(4,1)} %bitcast.58), calls=%async_computation.4 | async-start | bytes 524288
Sparse Core Ops, SparseCore 0:
  51.3 217.8 all-reduce.2
  315.9 68.1 all-gather.1
where the time goes:
time: 398 us; the launch traced here: 397 us
  waiting for transfers between devices  282 us (71%)
  local copies, waits for them, and re-layouts  48.1 us (12%)
  starting transfers between devices  20.1 us (5%)
  other arithmetic  17.9 us (4%)
  between operations  17.3 us (4%)
  matrix products  11.2 us (3%)
    psum x1, waiting for transfers between devices, spread(): return lax.psum(block, axis)  214 us
    all_gather x1, waiting for transfers between devices, on_device(): lax.all_gather(context, 'head', axis=1, tiled=True)  68.3 us
    slice x2, local copies, waits for them, and re-layouts, attend_sets(): key_part = pair_rows[..., :columns].reshape(block_count, -1, head_count, DH)  14.6 us
    all_to_all x1, starting transfers between devices, on_device(): lax.all_to_all(outgoing, 'seq', split_axis=0, concat_axis=0, tiled=True)  10.9 us
  transfers between devices with their start and end apart: 5, of which 2 were waited for; matrix products, arithmetic and copies ran while one was open for 3% of the time, Pallas kernels for 0%

commit v1 on v0

--- a/solution.py
+++ b/solution.py
@@ -1,3 +1,4 @@
+import functools
 from functools import reduce
 import math
 import jax
@@ -9,6 +10,36 @@
 BLOCK = 64
 R = 3
 G = 2
+
+
+def pack_ticks(array_in, chip_axis):
+    r2 = lax.axis_size(chip_axis)
+    f_now = lax.axis_index(chip_axis)
+    x_next, p_next, block_out = (r2, f_now, array_in.shape[1])
+    in_order = [q * x_next if d == 1 else q for d, q in enumerate(array_in.shape)]
+    tall = jnp.zeros(in_order, array_in.dtype)
+    later = found_now = array_in
+    y_new = lax.dynamic_update_slice_in_dim(tall, array_in, p_next * block_out, axis=1)
+    for idx in range(1, x_next // 2 + 1):
+        aux = range(x_next)
+        raw_out = map(lambda d: (d, (d + 1) % x_next), aux)
+        new = list(raw_out)
+        later = lax.ppermute(later, chip_axis, new)
+        y_new = lax.dynamic_update_slice_in_dim(
+            y_new, later, (p_next - idx) % x_next * block_out, axis=1
+        )
+        if 2 * idx < x_next:
+            side_arr = range(x_next)
+            local_out = map(lambda d: (d, (d - 1) % x_next), side_arr)
+            step_out = list(local_out)
+            found_now = lax.ppermute(found_now, chip_axis, step_out)
+            y_new = lax.dynamic_update_slice_in_dim(
+                y_new, found_now, (p_next + idx) % x_next * block_out, axis=1
+            )
+    return y_new
+
+
+mark_runs_on_mesh = functools.partial(pack_ticks, chip_axis="head")
 
 
 def padded_2(x, sides, width):
@@ -115,11 +146,7 @@
         per_device, -1, 2 * columns
     )
     context = attend_sets(query_rows, [joined_sets], columns)
-    summed = jnp.dot(
-        lax.all_gather(context, "head", axis=1, tiled=True),
-        w_out,
-        preferred_element_type=jnp.float32,
-    )
+    summed = jnp.dot(mark_runs_on_mesh(context), w_out, preferred_element_type=jnp.float32)
     return summed.astype(jnp.bfloat16)
 
 

time: 398 us -> 398 us (level)
  the two profiles are of different devices: /device:TPU:64 before, /device:TPU:2 now
where the time goes in v1:
time: 398 us; the launch traced here: 397 us
  waiting for transfers between devices  258 us (65%)
  local copies, waits for them, and re-layouts  51.8 us (13%)
  starting transfers between devices  42.8 us (11%)
  other arithmetic  17.9 us (4%)
  between operations  17.8 us (4%)
  matrix products  8.89 us (2%)
    psum x1, waiting for transfers between devices, spread(): return lax.psum(block, axis)  215 us
    ppermute x4, waiting for transfers between devices, pack_ticks(): later = lax.ppermute(later, chip_axis, new)  41.3 us
    slice x2, local copies, waits for them, and re-layouts, attend_sets(): key_part = pair_rows[..., :columns].reshape(block_count, -1, head_count, DH)  14.6 us
    ppermute x3, starting transfers between devices, pack_ticks(): found_now = lax.ppermute(found_now, chip_axis, step_out)  14.5 us
    all_to_all x1, starting transfers between devices, on_device(): lax.all_to_all(outgoing, 'seq', split_axis=0, concat_axis=0, tiled=True)  11.1 us
    ppermute x4, starting transfers between devices, pack_ticks(): later = lax.ppermute(later, chip_axis, new)  9.29 us
  transfers between devices with their start and end apart: 11, of which 7 were waited for; matrix products, arithmetic and copies ran while one was open for 4% of the time, Pallas kernels for 0%

profile of v1, /device:TPU:2, one launch (start us, length us, event | category | flops | bytes accessed | tf_op | source)
XLA Modules:
  0.0 396.6 jit_solution(11217484784528925267)
XLA Ops:
  6.5 0.9 compare_convert_fusion
  7.4 0.2 copy.53
  7.7 0.2 reshape.172
  7.9 0.2 reduce_window_sum.11
  8.2 0.1 copy.54
  8.3 1.0 copy.58
  9.3 0.2 broadcast_in_dim.66
  9.6 0.1 copy.61
  9.8 1.1 constant_dynamic-update-slice_fusion.1
  10.9 0.1 reshape.164
  11.1 0.1 copy.60
  11.2 0.1 copy.57
  11.3 1.1 constant_dynamic-update-slice_fusion
  12.4 6.6 %gather_fusion = bf16[128,64,512]{2,1,0:T(8,128)(2,1)} fusion(bf16[17,64,512]{2,1,0:T(8,128)(2,1)S(1)} %bitcast.54, s32[1024]{0:T(1024)S(1)} %pad_clamp_fusion.1), kind=kCustom, calls=%fused_computation | custom fusion | bytes 16777728 | tf_op jit(solution)/shard_map/jit(_take)/gather | solution.py:126
  19.0 7.5 %select_select_fusion = bf16[64,2,64,512]{3,2,1,0:T(8,128)(2,1)} fusion(bf16[64,2,64,512]{3,2,1,0:T(8,128)(2,1)} %bitcast.57, pred[64,2]{1,0:T(8,128)(4,1)S(1)} %copy.60, pred[64,2]{1,0:T(8,128)(4,1)S(1)} %copy.57), kind=kLoop, calls=%fused_computation.2 | loop fusion | flops 8388608 | bytes 16777472 | tf_op jit(solution)/shard_map/jit(_where)/select_n | solution.py:129
  26.5 11.1 %all-to-all-start = ((bf16[64,2,64,512]{3,2,1,0:T(8,128)(2,1)}), bf16[64,2,64,512]{3,2,1,0:T(8,128)(2,1)}, u32[]{:S(2)}, u32[]{:S(2)}) async-start(bf16[64,2,64,512]{3,2,1,0:T(8,128)(2,1)} %select_select_fusion), calls=%async_computation | async-start | bytes 16777216 | tf_op jit(solution)/shard_map/all_to_all | solution.py:130
  37.7 2.1 collective-permute-start
  39.7 5.8 %collective-permute-start.1 = (bf16[64,512]{1,0:T(8,128)(2,1)S(1)}, bf16[64,512]{1,0:T(8,128)(2,1)S(1)}, u32[]{:S(2)}, u32[]{:S(2)}) collective-permute-start(bf16[64,512]{1,0:T(8,128)(2,1)S(1)} %get-tuple-element.15), channel_id=1, source_target_pairs={{8,0},{16,8},{24,16},{32,24},{40,32},{48,40},{56,48},{64,56},{72,6... | collective-permute-start | bytes 196616 | tf_op jit(solution)/shard_map/ppermute | solution.py:53
  45.5 0.6 fusion.21
  50.1 0.7 dynamic-slice_select_fusion.1
  50.8 0.8 broadcast_multiply_fusion
  51.5 0.1 copy.50
  51.6 0.1 reshape.163
  51.7 0.1 copy.62
  51.8 0.1 mul.58
  51.9 0.2 convert_reduce_fusion
  52.2 0.1 copy.51
  52.3 0.1 copy.52
  52.4 2.5 reshape_reshape.3
  54.9 214.9 %all-reduce.3.cloned.1.call-done = (bf16[1,64,512]{2,1,0:T(8,128)(2,1)}, bf16[1,64,512]{2,1,0:T(8,128)(2,1)}) async-done(((bf16[1,64,512]{2,1,0:T(8,128)(2,1)}, bf16[1,64,512]{2,1,0:T(8,128)(2,1)}), (bf16[1,64,512]{2,1,0:T(8,128)(2,1)}, bf16[1,64,512]{2,1,0:T(8,128)(2,1)})) %all-reduce.3.cloned.1.call-update) | async-done | bytes 131088 | tf_op jit(solution)/shard_map/psum | solution.py:60
  269.8 0.9 pad_maximum_fusion.2
  270.7 0.2 pad_maximum_fusion
  270.9 1.0 constant_dynamic-update-slice_fusion.4
  271.9 1.1 constant_dynamic-update-slice_fusion.3
  273.0 1.1 constant_dynamic-update-slice_fusion.2
  274.1 1.6 broadcast_dynamic-update-slice_fusion
  275.7 5.9 %gather_fusion.1 = bf16[51,64,512]{2,1,0:T(8,128)(2,1)} fusion(bf16[128,64,512]{2,1,0:T(8,128)(2,1)} %bitcast.12, s32[1024]{0:T(1024)S(1)} %pad_clamp_fusion), kind=kCustom, calls=%fused_computation.1 | custom fusion | bytes 6684876 | tf_op jit(solution)/shard_map/jit(_take)/gather | solution.py:140
  281.6 5.1 %select_dynamic-update-slice_fusion = bf16[17,8,64,512]{3,2,1,0:T(8,128)(2,1)} fusion(bf16[17,8,64,512]{3,2,1,0:T(8,128)(2,1)} %broadcast_dynamic-update-slice_fusion, bf16[17,3,64,512]{3,2,1,0:T(8,128)(2,1)} %bitcast.59, pred[17,3]{1,0:T(8,128)(4,1)S(1)} %copy.52), kind=kLoop, calls=%fused_computation.8 | loop fusion | flops 1671168 | bytes 6684723 | tf_op jit(solution)/shard_map/concatenate | solution.py:145
  286.7 8.1 %fusion.19 = (bf16[17,512,256]{2,1,0:T(8,128)(2,1)}, bf16[17,512,256]{2,1,0:T(8,128)(2,1)}) fusion(bf16[17,512,512]{2,1,0:T(8,128)(2,1)} %bitcast.16), kind=kLoop, calls=%fused_computation.59 | loop fusion | bytes 17825792 | tf_op jit(solution)/shard_map/slice | solution.py:70
  294.8 6.5 %copy.64 = bf16[17,512,256]{1,2,0:T(8,128)(2,1)} copy(bf16[17,512,256]{2,1,0:T(8,128)(2,1)} %get-tuple-element.9) | data formatting | bytes 8912896 | tf_op jit(solution)/shard_map/slice | solution.py:70
  301.3 6.6 %copy.63 = bf16[17,512,256]{1,2,0:T(8,128)(2,1)} copy(bf16[17,512,256]{2,1,0:T(8,128)(2,1)} %get-tuple-element.10) | data formatting | bytes 8912896 | tf_op jit(solution)/shard_map/slice | solution.py:83
  307.9 3.4 bitcast_reduce_fusion
  311.3 1.3 fusion.1
  312.7 2.0 divide_convert_fusion
  314.7 0.6 copy.68
  315.4 3.6 collective-permute-start.2
  319.0 4.2 %collective-permute-start.3 = (bf16[1088,256]{1,0:T(8,128)(2,1)S(1)}, bf16[1088,256]{1,0:T(8,128)(2,1)}, u32[]{:S(2)}, u32[]{:S(2)}) collective-permute-start(bf16[1088,256]{1,0:T(8,128)(2,1)S(1)} %bitcast.68), channel_id=1, source_target_pairs={{0,7},{1,0},{2,1},{3,2},{4,3},{5,4},{6,5},{7,6},{8,15},{9,8},{10,9... | collective-permute-start | bytes 1671176 | tf_op jit(solution)/shard_map/ppermute | solution.py:35
  323.2 11.1 %collective-permute-done.2 = bf16[1088,256]{1,0:T(8,128)(2,1)} collective-permute-done((bf16[1088,256]{1,0:T(8,128)(2,1)S(1)}, bf16[1088,256]{1,0:T(8,128)(2,1)}, u32[]{:S(2)}, u32[]{:S(2)}) %collective-permute-start.2) | collective-permute-done | bytes 557088 | tf_op jit(solution)/shard_map/ppermute | solution.py:27
  334.3 1.9 collective-permute-start.4
  336.4 0.1 collective-permute-done.3
  336.4 5.1 %collective-permute-start.5 = (bf16[1088,256]{1,0:T(8,128)(2,1)}, bf16[1088,256]{1,0:T(8,128)(2,1)S(1)}, u32[]{:S(2)}, u32[]{:S(2)}) collective-permute-start(bf16[1088,256]{1,0:T(8,128)(2,1)} %collective-permute-done.3), channel_id=1, source_target_pairs={{0,7},{1,0},{2,1},{3,2},{4,3},{5,4},{6,5},{7,6},{8,15},{9,8},{10,9... | collective-permute-start | bytes 1671176 | tf_op jit(solution)/shard_map/ppermute | solution.py:35
  341.6 0.5 broadcast_in_dim.62
  342.1 0.1 constant_dynamic-update-slice_fusion.11
  342.3 10.3 %collective-permute-done.4 = bf16[1088,256]{1,0:T(8,128)(2,1)} collective-permute-done((bf16[1088,256]{1,0:T(8,128)(2,1)}, bf16[1088,256]{1,0:T(8,128)(2,1)}, u32[]{:S(2)}, u32[]{:S(2)}) %collective-permute-start.4) | collective-permute-done | bytes 557088 | tf_op jit(solution)/shard_map/ppermute | solution.py:27
  352.6 1.9 collective-permute-start.6
  354.5 1.1 constant_dynamic-update-slice_fusion.10
  355.6 1.1 constant_dynamic-update-slice_fusion.9
  356.8 5.1 %collective-permute-start.7 = (bf16[1088,256]{1,0:T(8,128)(2,1)S(1)}, bf16[1088,256]{1,0:T(8,128)(2,1)S(1)}, u32[]{:S(2)}, u32[]{:S(2)}) collective-permute-start(bf16[1088,256]{1,0:T(8,128)(2,1)S(1)} %collective-permute-done.5), channel_id=1, source_target_pairs={{0,7},{1,0},{2,1},{3,2},{4,3},{5,4},{6,5},{7,6},{8,15},{9,8},{10,9... | collective-permute-start | bytes 1671176 | tf_op jit(solution)/shard_map/ppermute | solution.py:35
  361.9 1.1 constant_dynamic-update-slice_fusion.8
  363.1 6.9 %collective-permute-done.6 = bf16[1088,256]{1,0:T(8,128)(2,1)S(1)} collective-permute-done((bf16[1088,256]{1,0:T(8,128)(2,1)}, bf16[1088,256]{1,0:T(8,128)(2,1)S(1)}, u32[]{:S(2)}, u32[]{:S(2)}) %collective-permute-start.6) | collective-permute-done | bytes 557088 | tf_op jit(solution)/shard_map/ppermute | solution.py:27
  370.0 1.9 collective-permute-start.8
  372.1 1.2 collective-permute-done.7
  373.3 12.9 %collective-permute-done.8 = bf16[1088,256]{1,0:T(8,128)(2,1)S(1)} collective-permute-done((bf16[1088,256]{1,0:T(8,128)(2,1)S(1)}, bf16[1088,256]{1,0:T(8,128)(2,1)S(1)}, u32[]{:S(2)}, u32[]{:S(2)}) %collective-permute-start.8) | collective-permute-done | bytes 557088 | tf_op jit(solution)/shard_map/ppermute | solution.py:27
  386.3 3.5 convolution_convert_fusion
  (36 shorter events, 0.9 us)
Async XLA Ops:
  6.5 379.8 %copy-start = (bf16[2048,512]{1,0:T(8,128)(2,1)S(1)}, bf16[2048,512]{1,0:T(8,128)(2,1)}, u32[]{:S(2)}) copy-start(bf16[2048,512]{1,0:T(8,128)(2,1)} %param.13) | copy-start | bytes 6291460
  26.5 19.0 %copy-start.2 = (s32[2]{0:T(128)S(1)}, s32[2]{0:T(128)}, u32[]{:S(2)}) copy-start(s32[2]{0:T(128)} %param.12) | copy-start | bytes 28
  26.5 249.2 %all-to-all-start = ((bf16[64,2,64,512]{3,2,1,0:T(8,128)(2,1)}), bf16[64,2,64,512]{3,2,1,0:T(8,128)(2,1)}, u32[]{:S(2)}, u32[]{:S(2)}) async-start(bf16[64,2,64,512]{3,2,1,0:T(8,128)(2,1)} %select_select_fusion), calls=%async_computation | async-start | bytes 16777216 | tf_op jit(solution)/shard_map/all_to_all | solution.py:130
  37.6 232.2 %all-reduce.3.cloned.1.call-start = ((), (), s32[]{:S(2)}) async-start(), calls=%async_computation.1 | async-start | bytes 262144 | tf_op jit(solution)/shard_map/psum | solution.py:60
  37.7 233.0 %collective-permute-start = (bf16[64,512]{1,0:T(8,128)(2,1)S(1)}, bf16[64,512]{1,0:T(8,128)(2,1)S(1)}, u32[]{:S(2)}, u32[]{:S(2)}) collective-permute-start(bf16[64,512]{1,0:T(8,128)(2,1)S(1)} %get-tuple-element.16), channel_id=1, source_target_pairs={{0,8},{8,16},{16,24},{24,32},{32,40},{40,48},{48,56},{56,64},{64,7... | collective-permute-start | bytes 196616 | tf_op jit(solution)/shard_map/ppermute | solution.py:52
  39.7 231.0 %collective-permute-start.1 = (bf16[64,512]{1,0:T(8,128)(2,1)S(1)}, bf16[64,512]{1,0:T(8,128)(2,1)S(1)}, u32[]{:S(2)}, u32[]{:S(2)}) collective-permute-start(bf16[64,512]{1,0:T(8,128)(2,1)S(1)} %get-tuple-element.15), channel_id=1, source_target_pairs={{8,0},{16,8},{24,16},{32,24},{40,32},{48,40},{56,48},{64,56},{72,6... | collective-permute-start | bytes 196616 | tf_op jit(solution)/shard_map/ppermute | solution.py:53
  301.3 6.7 %copy-start.1 = (bf16[17,64,2,128]{3,2,1,0:T(2,128)(2,1)S(1)}, bf16[17,64,2,128]{3,2,1,0:T(2,128)(2,1)}, u32[]{:S(2)}) copy-start(bf16[17,64,2,128]{3,2,1,0:T(2,128)(2,1)} %reshape_reshape.3) | copy-start | bytes 1671172
  307.9 4.8 %slice-start = ((s8[4456448]{0:T(1024)(128)(4,1)}), s8[4194304]{0:T(1024)(128)(4,1)S(1)}, s32[]{:S(2)}) async-start(s8[4456448]{0:T(1024)(128)(4,1)} %bitcast.62), calls=%async_computation.2 | async-start | bytes 8388608
  307.9 4.8 %slice-start.1 = ((s8[4456448]{0:T(1024)(128)(4,1)}), s8[262144]{0:T(1024)(128)(4,1)S(1)}, s32[]{:S(2)}) async-start(s8[4456448]{0:T(1024)(128)(4,1)} %bitcast.62), calls=%async_computation.3 | async-start | bytes 524288
  315.4 18.9 %collective-permute-start.2 = (bf16[1088,256]{1,0:T(8,128)(2,1)S(1)}, bf16[1088,256]{1,0:T(8,128)(2,1)}, u32[]{:S(2)}, u32[]{:S(2)}) collective-permute-start(bf16[1088,256]{1,0:T(8,128)(2,1)S(1)} %bitcast.67), channel_id=1, source_target_pairs={{0,1},{1,2},{2,3},{3,4},{4,5},{5,6},{6,7},{7,0},{8,9},{9,10},{10,1... | collective-permute-start | bytes 1671176 | tf_op jit(solution)/shard_map/ppermute | solution.py:27
  319.0 17.5 %collective-permute-start.3 = (bf16[1088,256]{1,0:T(8,128)(2,1)S(1)}, bf16[1088,256]{1,0:T(8,128)(2,1)}, u32[]{:S(2)}, u32[]{:S(2)}) collective-permute-start(bf16[1088,256]{1,0:T(8,128)(2,1)S(1)} %bitcast.68), channel_id=1, source_target_pairs={{0,7},{1,0},{2,1},{3,2},{4,3},{5,4},{6,5},{7,6},{8,15},{9,8},{10,9... | collective-permute-start | bytes 1671176 | tf_op jit(solution)/shard_map/ppermute | solution.py:35
  334.3 18.3 %collective-permute-start.4 = (bf16[1088,256]{1,0:T(8,128)(2,1)}, bf16[1088,256]{1,0:T(8,128)(2,1)}, u32[]{:S(2)}, u32[]{:S(2)}) collective-permute-start(bf16[1088,256]{1,0:T(8,128)(2,1)} %collective-permute-done.2), channel_id=1, source_target_pairs={{0,1},{1,2},{2,3},{3,4},{4,5},{5,6},{6,7},{7,0},{8,9},{9,10},{10,1... | collective-permute-start | bytes 1671176 | tf_op jit(solution)/shard_map/ppermute | solution.py:27
  336.4 20.3 %collective-permute-start.5 = (bf16[1088,256]{1,0:T(8,128)(2,1)}, bf16[1088,256]{1,0:T(8,128)(2,1)S(1)}, u32[]{:S(2)}, u32[]{:S(2)}) collective-permute-start(bf16[1088,256]{1,0:T(8,128)(2,1)} %collective-permute-done.3), channel_id=1, source_target_pairs={{0,7},{1,0},{2,1},{3,2},{4,3},{5,4},{6,5},{7,6},{8,15},{9,8},{10,9... | collective-permute-start | bytes 1671176 | tf_op jit(solution)/shard_map/ppermute | solution.py:35
  352.6 17.4 %collective-permute-start.6 = (bf16[1088,256]{1,0:T(8,128)(2,1)}, bf16[1088,256]{1,0:T(8,128)(2,1)S(1)}, u32[]{:S(2)}, u32[]{:S(2)}) collective-permute-start(bf16[1088,256]{1,0:T(8,128)(2,1)} %collective-permute-done.4), channel_id=1, source_target_pairs={{0,1},{1,2},{2,3},{3,4},{4,5},{5,6},{6,7},{7,0},{8,9},{9,10},{10,1... | collective-permute-start | bytes 1671176 | tf_op jit(solution)/shard_map/ppermute | solution.py:27
  356.8 16.4 %collective-permute-start.7 = (bf16[1088,256]{1,0:T(8,128)(2,1)S(1)}, bf16[1088,256]{1,0:T(8,128)(2,1)S(1)}, u32[]{:S(2)}, u32[]{:S(2)}) collective-permute-start(bf16[1088,256]{1,0:T(8,128)(2,1)S(1)} %collective-permute-done.5), channel_id=1, source_target_pairs={{0,7},{1,0},{2,1},{3,2},{4,3},{5,4},{6,5},{7,6},{8,15},{9,8},{10,9... | collective-permute-start | bytes 1671176 | tf_op jit(solution)/shard_map/ppermute | solution.py:35
  370.0 16.3 %collective-permute-start.8 = (bf16[1088,256]{1,0:T(8,128)(2,1)S(1)}, bf16[1088,256]{1,0:T(8,128)(2,1)S(1)}, u32[]{:S(2)}, u32[]{:S(2)}) collective-permute-start(bf16[1088,256]{1,0:T(8,128)(2,1)S(1)} %collective-permute-done.6), channel_id=1, source_target_pairs={{0,1},{1,2},{2,3},{3,4},{4,5},{5,6},{6,7},{7,0},{8,9},{9,10},{10,1... | collective-permute-start | bytes 1671176 | tf_op jit(solution)/shard_map/ppermute | solution.py:27
Sparse Core Ops, SparseCore 0:
  50.9 218.8 all-reduce.2
